TPU v7x, 32 devices: a whole 2x2x4 slice. The times are simulated.
32 devices in a mesh: dp: 4 (over x, core), expert: 2 (over y), tensor: 4 (over z).
Axes of the slice: x: 2, y: 2, z: 4, core: 2. Of those that a mesh axis runs over, the one named last changes fastest.
Arguments:
- tokens: bfloat16 [8, 256, 2048], P(('dp', 'expert')), may hold values from -6 to 6
- cotangent: bfloat16 [8, 256, 2048], P(('dp', 'expert')), may hold values from -6 to 6
- head_counts: int32 [8], P(('dp', 'expert')), may hold values from 4 to 16, as said below
- positions: int32 [8, 256], P(('dp', 'expert')), may hold values from 0 to 255, as said below
- buckets: int32 [8, 256], P(('dp', 'expert')), may hold values from 0 to 3, as said below
- in_master: float32 [3, 2048, 2048], P(None, ('dp', 'expert'), 'tensor'), may hold values from -0.13258252 to 0.13258252
- out_master: float32 [2048, 2048], P('tensor', ('dp', 'expert')), may hold values from -1.5 to 1.5
- up_master: float32 [4, 2048, 2048], P(None, ('dp', 'expert'), 'tensor'), may hold values from -0.13258252 to 0.13258252
- down_master: float32 [4, 2048, 2048], P(None, 'tensor', ('dp', 'expert')), may hold values from -0.06629126 to 0.06629126
- norm_master: float32 [4, 2048], P(None, ('dp', 'expert')), may hold values from -0.6 to 2.4
- in_first: float32 [3, 2048, 2048], P(None, ('dp', 'expert'), 'tensor'), may hold values from -32 to 32
- out_first: float32 [2048, 2048], P('tensor', ('dp', 'expert')), may hold values from -6 to 6
- up_first: float32 [4, 2048, 2048], P(None, ('dp', 'expert'), 'tensor'), may hold values from -16 to 16
- down_first: float32 [4, 2048, 2048], P(None, 'tensor', ('dp', 'expert')), may hold values from -28 to 28
- norm_first: float32 [4, 2048], P(None, ('dp', 'expert')), may hold values from -32 to 32
- in_second: float32 [3, 2048, 2048], P(None, ('dp', 'expert'), 'tensor'), may hold values from 1.024 to 16.384
- out_second: float32 [2048, 2048], P('tensor', ('dp', 'expert')), may hold values from 0.0065536 to 0.1048576
- up_second: float32 [4, 2048, 2048], P(None, ('dp', 'expert'), 'tensor'), may hold values from 0.3072 to 4.9152
- down_second: float32 [4, 2048, 2048], P(None, 'tensor', ('dp', 'expert')), may hold values from 0.9216 to 14.7456
- norm_second: float32 [4, 2048], P(None, ('dp', 'expert')), may hold values from 1.024 to 16.384
Outputs:
- output: float32 [8, 256, 2048], P(('dp', 'expert'))
- input_grad: float32 [8, 256, 2048], P(('dp', 'expert'))
- bucket_share: float32 [4], replicated
- lamb_norms: float32 [2, 8], replicated
- in_weight: float32 [3, 2048, 2048], P(None, ('dp', 'expert'), 'tensor')
- out_weight: float32 [2048, 2048], P('tensor', ('dp', 'expert'))
- up_weight: float32 [4, 2048, 2048], P(None, ('dp', 'expert'), 'tensor')
- down_weight: float32 [4, 2048, 2048], P(None, 'tensor', ('dp', 'expert'))
- norm_weight: float32 [4, 2048], P(None, ('dp', 'expert'))
- in_moment: float32 [3, 2048, 2048], P(None, ('dp', 'expert'), 'tensor')
- out_moment: float32 [2048, 2048], P('tensor', ('dp', 'expert'))
- up_moment: float32 [4, 2048, 2048], P(None, ('dp', 'expert'), 'tensor')
- down_moment: float32 [4, 2048, 2048], P(None, 'tensor', ('dp', 'expert'))
- norm_moment: float32 [4, 2048], P(None, ('dp', 'expert'))
- in_square: float32 [3, 2048, 2048], P(None, ('dp', 'expert'), 'tensor')
- out_square: float32 [2048, 2048], P('tensor', ('dp', 'expert'))
- up_square: float32 [4, 2048, 2048], P(None, ('dp', 'expert'), 'tensor')
- down_square: float32 [4, 2048, 2048], P(None, 'tensor', ('dp', 'expert'))
- norm_square: float32 [4, 2048], P(None, ('dp', 'expert'))
Inputs may be any that keep to these rules, and one draw needn't show every extreme that they name: `head_counts`: each is a whole multiple of a quarter of 16. Within each sequence positions count up by one from 0 and restart at 0 at a document's first token; each sequence's first token has position 0. `buckets`: in each sequence no bucket id is carried by more than 80 tokens; one bucket id, the same for all sequences, is carried by exactly 80 tokens of every sequence.
All inputs are finite; a program needn't handle non-finite values.
Results may differ from a plain program's by a relative error of at most 0.014.
The roundings to bfloat16 on the way count: a program that leaves them out, or rounds other values in their place, can miss the bound.
Values may be sent and summed in bfloat16 or wider, within the bound.
A program may use at most 448 MiB of HBM per device.

v0:
```python
import math

import jax
import jax.numpy as jnp
from jax import lax
from jax.experimental import pallas as pl
from jax.experimental.pallas import tpu as pltpu
from jax.sharding import PartitionSpec as P

HEAD_DIM = 128
STEP = 10


NORM_EPS = 1e-05
BETA_FIRST = 0.9
BETA_SECOND = 0.999
ADAM_EPS = 1e-06
WEIGHT_DECAY = 0.01
LEARN_RATE = 0.25
MASKED = -1e30
ROPE_BASE = 10000.0


def layer_norm(values, gain_row, shift_row):
    center = values - jnp.mean(values, -1, keepdims=True)
    variance = jnp.mean(center * center, -1, keepdims=True)
    inv_std = lax.rsqrt(variance + NORM_EPS)
    normed = center * inv_std
    return (normed * gain_row + shift_row, normed, inv_std)


def norm_back_rows(grad_out, normed, inv_std, gain_row):
    scaled = grad_out * gain_row
    inner_part = (
        scaled
        - jnp.mean(scaled, -1, keepdims=True)
        - normed * jnp.mean(scaled * normed, -1, keepdims=True)
    )
    return (inner_part * inv_std, jnp.sum(grad_out * normed, 0), jnp.sum(grad_out, 0))


def rope_angles(position_row):
    freq_index = jnp.arange(HEAD_DIM // 2, dtype=jnp.float32)
    inverse = jnp.exp(freq_index * (-2.0 * jnp.log(ROPE_BASE) / HEAD_DIM))
    return position_row.astype(jnp.float32)[:, None] * inverse[None, :]


def rotary(values, angles, sign_value):
    half_dim = values.shape[-1] // 2
    cosine = jnp.cos(angles)[:, None, :]
    sine_part = sign_value * jnp.sin(angles)[:, None, :]
    first_half = values[..., :half_dim]
    second_half = values[..., half_dim:]
    return jnp.concatenate(
        [
            first_half * cosine - second_half * sine_part,
            second_half * cosine + first_half * sine_part,
        ],
        -1,
    )


def block_mask(key_index, position_row, block_start, block_rows):
    query_index = block_start + jnp.arange(block_rows, dtype=jnp.int32)
    return (key_index[None, :] <= query_index[:, None]) & (
        key_index[None, :] >= (query_index - position_row)[:, None]
    )


def attend_forward(queries, key_rows, value_rows, position_row, block_rows):
    length = queries.shape[0]
    key_index = jnp.arange(length, dtype=jnp.int32)

    def one_block(block_start):
        allowed = block_mask(key_index, position_row, block_start, block_rows)
        scores = jnp.einsum("qhd,khd->hqk", queries, key_rows, preferred_element_type=jnp.float32)
        scores = jnp.where(allowed[None], scores, MASKED)
        row_peak = jnp.max(scores, -1, keepdims=True)
        exp_scores = jnp.exp(scores - row_peak)
        row_total = jnp.sum(exp_scores, -1, keepdims=True)
        attn_weights = (exp_scores / row_total).astype(jnp.bfloat16)
        block_out = jnp.einsum(
            "hqk,khd->qhd", attn_weights, value_rows, preferred_element_type=jnp.float32
        )
        return (block_out, row_peak[..., 0] + jnp.log(row_total[..., 0]))

    starts = jnp.arange(length // block_rows, dtype=jnp.int32) * block_rows
    block_outs, log_totals = lax.map(one_block, starts)
    return (block_outs.reshape(queries.shape), log_totals, starts)


def attend_backward(
    queries, key_rows, value_rows, position_row, grad_heads, log_totals, starts, block_rows
):
    length = queries.shape[0]
    key_index = jnp.arange(length, dtype=jnp.int32)

    def one_block(carried, inputs):
        block_start, block_log = inputs
        allowed = block_mask(key_index, position_row, block_start, block_rows)
        scores = jnp.einsum("qhd,khd->hqk", queries, key_rows, preferred_element_type=jnp.float32)
        scores = jnp.where(allowed[None], scores, MASKED)
        attn_probs = jnp.exp(scores - block_log[..., None])
        grad_probs = jnp.einsum(
            "qhd,khd->hqk", grad_heads, value_rows, preferred_element_type=jnp.float32
        )
        row_inner = jnp.sum(attn_probs * grad_probs, -1, keepdims=True)
        grad_scores = (attn_probs * (grad_probs - row_inner)).astype(jnp.bfloat16)
        grad_query = jnp.einsum(
            "hqk,khd->qhd", grad_scores, key_rows, preferred_element_type=jnp.float32
        )
        grad_keys = carried[0] + jnp.einsum(
            "hqk,qhd->khd", grad_scores, queries, preferred_element_type=jnp.float32
        )
        grad_values = carried[1] + jnp.einsum(
            "hqk,qhd->khd",
            attn_probs.astype(jnp.bfloat16),
            grad_heads,
            preferred_element_type=jnp.float32,
        )
        return ((grad_keys, grad_values), grad_query)

    start_state = (jnp.zeros(key_rows.shape, jnp.float32), jnp.zeros(value_rows.shape, jnp.float32))
    (grad_keys, grad_values), grad_query = lax.scan(one_block, start_state, (starts, log_totals))
    return (grad_query.reshape(queries.shape), grad_keys, grad_values)


def gather_rows(values, source_rows):
    padded = jnp.concatenate([values, jnp.zeros((1, values.shape[1]), values.dtype)], 0)
    return padded[source_rows]


def ffn_forward(rows_in, bucket, up_work, down_work):
    row_count = rows_in.shape[0]
    mixed_sum = jnp.zeros((row_count, down_work.shape[2]), jnp.float32)
    hiddens = []
    for quarter in range(4):

        def live_part():
            hidden = jnp.dot(rows_in, up_work[quarter], preferred_element_type=jnp.float32)
            squared = jnp.square(jnp.maximum(hidden, 0.0)).astype(jnp.bfloat16)
            return (
                hidden,
                jnp.dot(squared, down_work[quarter], preferred_element_type=jnp.float32),
            )

        def dead_part():
            return (
                jnp.zeros((row_count, up_work.shape[2]), jnp.float32),
                jnp.zeros_like(mixed_sum),
            )

        hidden, contribution = lax.cond(bucket >= quarter, live_part, dead_part)
        hiddens.append(hidden)
        mixed_sum = mixed_sum + contribution
    return (mixed_sum, hiddens)


def ffn_backward(rows_in, grads_in, bucket, hiddens, up_work, down_work):
    grad_rows = jnp.zeros((rows_in.shape[0], up_work.shape[1]), jnp.float32)
    grad_up = []
    grad_down = []
    for quarter in range(4):
        hidden = hiddens[quarter]

        def live_part():
            rectified = jnp.maximum(hidden, 0.0)
            squared = jnp.square(rectified).astype(jnp.bfloat16)
            grad_square = jnp.einsum(
                "rd,ud->ru", grads_in, down_work[quarter], preferred_element_type=jnp.float32
            )
            grad_hidden = (grad_square * 2.0 * rectified).astype(jnp.bfloat16)
            return (
                jnp.einsum("rd,ru->du", rows_in, grad_hidden, preferred_element_type=jnp.float32),
                jnp.einsum("ru,rd->ud", squared, grads_in, preferred_element_type=jnp.float32),
                jnp.einsum(
                    "ru,du->rd", grad_hidden, up_work[quarter], preferred_element_type=jnp.float32
                ),
            )

        def dead_part():
            return (
                jnp.zeros(up_work.shape[1:], jnp.float32),
                jnp.zeros(down_work.shape[1:], jnp.float32),
                jnp.zeros_like(grad_rows),
            )

        part_up, part_down, part_rows = lax.cond(bucket >= quarter, live_part, dead_part)
        grad_up.append(part_up)
        grad_down.append(part_down)
        grad_rows = grad_rows + part_rows
    return (grad_rows, jnp.stack(grad_up), jnp.stack(grad_down))


def ffn_total(partial_value):
    return lax.psum(partial_value, "tensor")


def ffn_grad_total(partial_value):
    return lax.psum(partial_value, "tensor")


def adam_terms(weight, gradient, first_old, second_old):
    first_new = BETA_FIRST * first_old + (1.0 - BETA_FIRST) * gradient
    second_new = BETA_SECOND * second_old + (1.0 - BETA_SECOND) * gradient * gradient
    update = (
        first_new
        / (1.0 - BETA_FIRST**STEP)
        / (jnp.sqrt(second_new / (1.0 - BETA_SECOND**STEP)) + ADAM_EPS)
        + WEIGHT_DECAY * weight
    )
    return (update, first_new, second_new)


def finish(output, input_grad, bucket_share, masters, firsts, seconds, grad_shards, tensor_count):
    norm_master = masters[4]
    adam_out = [
        adam_terms(masters[member], grad_shards[member], firsts[member], seconds[member])
        for member in range(5)
    ]
    weight_sq = jnp.concatenate(
        [
            jnp.stack([jnp.sum(masters[member] * masters[member]) for member in range(4)]),
            jnp.sum(norm_master * norm_master, 1) / tensor_count,
        ]
    )
    update_sq = jnp.concatenate(
        [
            jnp.stack([jnp.sum(adam_out[member][0] * adam_out[member][0]) for member in range(4)]),
            jnp.sum(adam_out[4][0] * adam_out[4][0], 1) / tensor_count,
        ]
    )
    weight_tot, update_tot = lax.psum((weight_sq, update_sq), ("dp", "expert", "tensor"))
    weight_norms = jnp.sqrt(weight_tot)
    update_norms = jnp.sqrt(update_tot)
    ratios = weight_norms / update_norms
    new_weights = [
        masters[member] - LEARN_RATE * ratios[member] * adam_out[member][0] for member in range(4)
    ]
    norm_new = norm_master - LEARN_RATE * ratios[4:, None] * adam_out[4][0]
    lamb_norms = jnp.stack([weight_norms, update_norms])
    return (
        output[None],
        input_grad[None],
        bucket_share,
        lamb_norms,
        new_weights[0],
        new_weights[1],
        new_weights[2],
        new_weights[3],
        norm_new,
        adam_out[0][1],
        adam_out[1][1],
        adam_out[2][1],
        adam_out[3][1],
        adam_out[4][1],
        adam_out[0][2],
        adam_out[1][2],
        adam_out[2][2],
        adam_out[3][2],
        adam_out[4][2],
    )


def body(
    tokens,
    cotangent,
    head_counts,
    positions,
    buckets,
    in_master,
    out_master,
    up_master,
    down_master,
    norm_master,
    in_first,
    out_first,
    up_first,
    down_first,
    norm_first,
    in_second,
    out_second,
    up_second,
    down_second,
    norm_second,
):
    in_work, out_work, up_work, down_work, norm_work = (
        lax.all_gather(in_master.astype(jnp.bfloat16), ("dp", "expert"), axis=1, tiled=True),
        lax.all_gather(out_master.astype(jnp.bfloat16), ("dp", "expert"), axis=1, tiled=True),
        lax.all_gather(up_master.astype(jnp.bfloat16), ("dp", "expert"), axis=1, tiled=True),
        lax.all_gather(down_master.astype(jnp.bfloat16), ("dp", "expert"), axis=2, tiled=True),
        lax.all_gather(norm_master.astype(jnp.bfloat16), ("dp", "expert"), axis=1, tiled=True),
    )
    length = tokens.shape[1]
    model_width = tokens.shape[2]
    heads_here = in_work.shape[2] // HEAD_DIM
    block_rows = min(512, length)
    head_scale = HEAD_DIM ** (-0.5)
    groups_data = lax.axis_size("dp") * lax.axis_size("expert")
    tensor_count = lax.axis_size("tensor")
    experts = lax.axis_size("expert")
    norm_gains = norm_work.astype(jnp.float32)
    inputs = tokens[0].astype(jnp.float32)
    first_norm, first_hat, first_inv = layer_norm(inputs, norm_gains[0], norm_gains[1])
    first_in = first_norm.astype(jnp.bfloat16)
    projected = jnp.einsum("td,jde->jte", first_in, in_work, preferred_element_type=jnp.float32)
    projected = projected.reshape(3, length, heads_here, HEAD_DIM)
    angles = rope_angles(positions[0])
    queries = (rotary(projected[0], angles, 1.0) * head_scale).astype(jnp.bfloat16)
    key_rows = rotary(projected[1], angles, 1.0).astype(jnp.bfloat16)
    value_rows = projected[2].astype(jnp.bfloat16)
    head_ids = lax.axis_index("tensor") * heads_here + jnp.arange(heads_here, dtype=jnp.int32)
    active = (head_ids < head_counts[0]).astype(jnp.float32)
    head_outs, log_totals, starts = attend_forward(
        queries, key_rows, value_rows, positions[0], block_rows
    )
    attended = (
        (head_outs * active[None, :, None])
        .astype(jnp.bfloat16)
        .reshape(length, heads_here * HEAD_DIM)
    )
    attn_part = jnp.dot(attended, out_work, preferred_element_type=jnp.float32)
    middle = inputs + lax.psum(attn_part, "tensor")
    second_norm, second_hat, second_inv = layer_norm(middle, norm_gains[2], norm_gains[3])
    second_in = second_norm.astype(jnp.bfloat16)
    bucket_ids = buckets[0]
    onehot = (bucket_ids[:, None] == jnp.arange(4, dtype=jnp.int32)[None, :]).astype(jnp.int32)
    bucket_rank = jnp.sum((jnp.cumsum(onehot, 0) - onehot) * onehot, 1)
    local_counts = jnp.sum(onehot, 0).astype(jnp.float32)
    bucket_share = lax.psum(local_counts, ("dp", "expert")) / (length * groups_data)
    most_rows = 5 * length // 16
    owner_group = max(experts // 4, 1)
    per_owner = max(4 // experts, 1)
    slot_rows = (most_rows + owner_group - 1) // owner_group
    capacity = per_owner * slot_rows
    slot_of = (
        (bucket_ids // per_owner * owner_group + bucket_rank % owner_group) * capacity
        + bucket_ids % per_owner * slot_rows
        + bucket_rank // owner_group
    )
    slot_total = experts * capacity
    source_rows = (
        jnp.full((slot_total,), length, jnp.int32)
        .at[slot_of]
        .set(jnp.arange(length, dtype=jnp.int32))
    )
    outgoing = gather_rows(second_in, source_rows).reshape(experts, capacity, model_width)
    incoming = lax.all_to_all(outgoing, "expert", split_axis=0, concat_axis=0, tiled=True).reshape(
        experts, per_owner, slot_rows, model_width
    )
    owner_index = lax.axis_index("expert")
    owned_ids = [owner_index // owner_group * per_owner + member for member in range(per_owner)]
    ffn_inputs = [
        incoming[:, member].reshape(experts * slot_rows, model_width) for member in range(per_owner)
    ]
    results = [
        ffn_forward(ffn_inputs[member], owned_ids[member], up_work, down_work)
        for member in range(per_owner)
    ]
    partial_value = jnp.stack(
        [
            results[member][0].reshape(experts, slot_rows, model_width)
            for member in range(per_owner)
        ],
        1,
    )
    summed = ffn_total(partial_value.reshape(experts, capacity, model_width)).astype(jnp.bfloat16)
    returned = lax.all_to_all(summed, "expert", split_axis=0, concat_axis=0, tiled=True)
    branch_out = returned.reshape(slot_total, model_width)[slot_of]
    output = middle + branch_out.astype(jnp.float32)
    grad_branch = cotangent[0]
    outgoing_grad = gather_rows(grad_branch, source_rows).reshape(experts, capacity, model_width)
    incoming_grad = lax.all_to_all(
        outgoing_grad, "expert", split_axis=0, concat_axis=0, tiled=True
    ).reshape(experts, per_owner, slot_rows, model_width)
    ffn_grads = [
        incoming_grad[:, member].reshape(experts * slot_rows, model_width)
        for member in range(per_owner)
    ]
    back_parts = [
        ffn_backward(
            ffn_inputs[member],
            ffn_grads[member],
            owned_ids[member],
            results[member][1],
            up_work,
            down_work,
        )
        for member in range(len(owned_ids))
    ]
    grad_up = back_parts[0][1]
    grad_down = back_parts[0][2]
    for member in range(1, len(owned_ids)):
        grad_up = grad_up + back_parts[member][1]
        grad_down = grad_down + back_parts[member][2]
    rows_back = jnp.stack(
        [
            back_parts[member][0].reshape(experts, slot_rows, model_width)
            for member in range(per_owner)
        ],
        1,
    )
    summed_back = ffn_grad_total(rows_back.reshape(experts, capacity, model_width)).astype(
        jnp.bfloat16
    )
    returned_back = lax.all_to_all(summed_back, "expert", split_axis=0, concat_axis=0, tiled=True)
    grad_second = returned_back.reshape(slot_total, model_width)[slot_of].astype(jnp.float32)
    grad_mid_norm, gain_second, shift_second = norm_back_rows(
        grad_second, second_hat, second_inv, norm_gains[2]
    )
    grad_middle = grad_branch.astype(jnp.float32) + grad_mid_norm
    grad_attn = grad_middle.astype(jnp.bfloat16)
    grad_attended = jnp.einsum("td,ed->te", grad_attn, out_work, preferred_element_type=jnp.float32)
    grad_out_w = jnp.einsum("te,td->ed", attended, grad_attn, preferred_element_type=jnp.float32)
    grad_heads = (
        grad_attended.astype(jnp.bfloat16).reshape(length, heads_here, HEAD_DIM)
        * active.astype(jnp.bfloat16)[None, :, None]
    )
    grad_query, grad_keys, grad_values = attend_backward(
        queries, key_rows, value_rows, positions[0], grad_heads, log_totals, starts, block_rows
    )
    grad_projected = jnp.stack(
        [
            rotary(grad_query * head_scale, angles, -1.0),
            rotary(grad_keys, angles, -1.0),
            grad_values,
        ]
    )
    grad_projected = grad_projected.reshape(3, length, heads_here * HEAD_DIM).astype(jnp.bfloat16)
    grad_in_w = jnp.einsum(
        "td,jte->jde", first_in, grad_projected, preferred_element_type=jnp.float32
    )
    grad_first_part = jnp.einsum(
        "jte,jde->td", grad_projected, in_work, preferred_element_type=jnp.float32
    )
    grad_first = lax.psum(grad_first_part, "tensor")
    grad_input_norm, gain_first, shift_first = norm_back_rows(
        grad_first, first_hat, first_inv, norm_gains[0]
    )
    input_grad = grad_middle + grad_input_norm
    grad_norm = jnp.stack([gain_first, shift_first, gain_second, shift_second])
    in_sum, out_sum, up_sum, down_sum, norm_sum = (
        lax.psum_scatter(grad_in_w, ("dp", "expert"), scatter_dimension=1, tiled=True),
        lax.psum_scatter(grad_out_w, ("dp", "expert"), scatter_dimension=1, tiled=True),
        lax.psum_scatter(grad_up, ("dp", "expert"), scatter_dimension=1, tiled=True),
        lax.psum_scatter(grad_down, ("dp", "expert"), scatter_dimension=2, tiled=True),
        lax.psum_scatter(grad_norm, ("dp", "expert"), scatter_dimension=1, tiled=True),
    )
    masters = (in_master, out_master, up_master, down_master, norm_master)
    firsts = (in_first, out_first, up_first, down_first, norm_first)
    seconds = (in_second, out_second, up_second, down_second, norm_second)
    grad_shards = (in_sum, out_sum, up_sum, down_sum, norm_sum)
    return finish(output, input_grad, bucket_share, masters, firsts, seconds, grad_shards, tensor_count)


MESH = pl.DeviceIdType.MESH
ANY = pl.BlockSpec(memory_space=pl.ANY)
VM = pl.BlockSpec(memory_space=pltpu.VMEM)
SM = pl.BlockSpec(memory_space=pltpu.SMEM)

F32 = jnp.float32
BF16 = jnp.bfloat16
CHUNK = 256
HALF = 128
ROWS = 64


class Here:
    def __init__(self):
        d = lax.axis_index("dp")
        self.x, self.c = d // 2, lax.rem(d, 2)
        self.y = lax.axis_index("expert")
        self.z = lax.axis_index("tensor")

    def plane(self, dx, dc, dy):
        x = 1 - self.x if dx else self.x
        c = 1 - self.c if dc else self.c
        y = 1 - self.y if dy else self.y
        return (x * 2 + c, y, self.z)

    def chunk(self, dx, dc, dy):
        x = 1 - self.x if dx else self.x
        c = 1 - self.c if dc else self.c
        y = 1 - self.y if dy else self.y
        return (x * 2 + c) * 2 + y

    def chunk_of(self, dx, dy, core):
        x = 1 - self.x if dx else self.x
        y = 1 - self.y if dy else self.y
        return (x * 2 + core) * 2 + y

    def along(self, step):
        return (self.x * 2 + self.c, self.y, lax.rem(self.z + step, 4))

    def behind(self, step):
        return lax.rem(self.z + 4 - step, 4)


PARTNER = (0, 1, 0)
PLANE = [(a, b, g) for a in (0, 1) for b in (0, 1) for g in (0, 1) if a + b + g > 0]
SIDES = [(1, 0, 0), (1, 1, 0), (0, 0, 1), (0, 1, 1)]


def greet(here, plane_peers, tensor_peers):
    barrier = pltpu.get_barrier_semaphore()
    for peer in plane_peers:
        pl.semaphore_signal(barrier, inc=1, device_id=here.plane(*peer), device_id_type=MESH)
    for step in tensor_peers:
        pl.semaphore_signal(barrier, inc=1, device_id=here.along(step), device_id_type=MESH)
    pl.semaphore_wait(barrier, len(plane_peers) + len(tensor_peers))


def push(src, dst, send, recv, device):
    copy = pltpu.make_async_remote_copy(
        src_ref=src, dst_ref=dst, send_sem=send, recv_sem=recv, device_id=device, device_id_type=MESH
    )
    copy.start()
    return copy


def block(index, size):
    return pl.ds(pl.multiple_of(index * size, size), size)


def rows_chunk(ref, k):
    return ref.at[:, block(k, CHUNK), :]


def rows_part(ref, k, part):
    return ref.at[:, pl.ds(pl.multiple_of(k * CHUNK + part * HALF, HALF), HALF), :]


def cols_chunk(ref, k):
    return ref.at[:, :, block(k, CHUNK)]


def cols_part(ref, k, part):
    return ref.at[:, part * HALF : part * HALF + HALF, block(k, CHUNK)]


class Gather:
    def __init__(self, here, by_rows, shard, whole, first, relay, local):
        self.here, self.by_rows, self.shard, self.whole = here, by_rows, shard, whole
        self.first, self.relay, self.local = first, relay, local
        self.copies = []

    def half(self, core):
        if self.by_rows:
            return self.shard.at[:, :, block(core, CHUNK)]
        return self.shard.at[:, block(core, CHUNK), :]

    def chunk(self, k):
        return rows_chunk(self.whole, k) if self.by_rows else cols_chunk(self.whole, k)

    def part(self, k, part):
        return rows_part(self.whole, k, part) if self.by_rows else cols_part(self.whole, k, part)

    def start(self):
        here = self.here
        mine = self.chunk(here.chunk(0, 0, 0))
        for index, side in enumerate(SIDES + [PARTNER]):
            core = 1 - here.c if side[1] else here.c
            self.copies.append(
                push(
                    self.half(core),
                    mine,
                    self.first.at[0, index],
                    self.first.at[1, index],
                    here.plane(*side),
                )
            )
        self.own = pltpu.make_async_copy(self.half(here.c), mine, self.local)
        self.own.start()

    def forward(self):
        here = self.here
        self.onward = []
        for index in range(4):
            side = SIDES[index]
            self.copies[index].wait_recv()
            part = 0 if side[0] else 1
            where = self.part(here.chunk(*side), part)
            target = (0, 0, 1) if side[0] else (1, 0, 0)
            self.onward.append(
                push(
                    where,
                    where,
                    self.relay.at[0, index],
                    self.relay.at[1, index],
                    here.plane(*target),
                )
            )

    def finish(self):
        for index in range(4):
            self.copies[index].wait_send()
        self.copies[4].wait()
        self.own.wait()
        for copy in self.onward:
            copy.wait()


def gather_sems():
    return [
        pltpu.SemaphoreType.DMA((2, 5)),
        pltpu.SemaphoreType.DMA((2, 4)),
        pltpu.SemaphoreType.DMA,
    ]


class Scatter:
    def __init__(self, here, by_rows, grad, total, bufs):
        self.here, self.by_rows, self.grad, self.total = here, by_rows, grad, total
        self.got, self.got_two = bufs[:2]
        self.one_sem, self.two_sem, self.last_sem, self.local = bufs[2:6]
        self.final = bufs[6]

    def part(self, dx, dy, core, side):
        k = self.here.chunk_of(dx, dy, core)
        return rows_part(self.grad, k, side) if self.by_rows else cols_part(self.grad, k, side)

    def start(self):
        here = self.here
        self.first = []
        for side in (0, 1):
            near, far = ((1, 0), (1, 1)) if side == 0 else ((0, 1), (1, 1))
            target = here.plane(1, 0, 0) if side == 0 else here.plane(0, 0, 1)
            for slot in range(4):
                chip = far if slot >= 2 else near
                index = side * 4 + slot
                self.first.append(
                    push(
                        self.part(chip[0], chip[1], slot % 2, side),
                        self.got.at[index],
                        self.one_sem.at[0, index],
                        self.one_sem.at[1, index],
                        target,
                    )
                )

    def middle(self):
        here = self.here
        self.second = []
        for side in (0, 1):
            target = here.plane(0, 0, 1) if side == 0 else here.plane(1, 0, 0)
            chip = (0, 1) if side == 0 else (1, 0)
            for slot in (2, 3):
                index = side * 4 + slot
                two = side * 2 + slot - 2
                mine = self.part(chip[0], chip[1], slot - 2, side)
                self.first[index].wait_recv()
                got = self.got.at[index]

                def step(i, carry):
                    spot = (i // 4, block(lax.rem(i, 4), 32), slice(None))
                    mine[spot] = (mine[spot].astype(F32) + got[spot].astype(F32)).astype(BF16)
                    return carry

                lax.fori_loop(0, got.shape[0] * 4, step, 0)
                self.second.append(
                    push(
                        mine,
                        self.got_two.at[two],
                        self.two_sem.at[0, two],
                        self.two_sem.at[1, two],
                        target,
                    )
                )

    def last(self):
        here = self.here
        for side in (0, 1):
            for slot in (0, 1):
                index = side * 4 + slot
                two = side * 2 + slot
                self.first[index].wait_recv()
                self.second[two].wait_recv()
                mine, got, got_two = self.part(0, 0, slot, side), self.got.at[index], self.got_two.at[two]
                final = self.final.at[slot, :, side * HALF : side * HALF + HALF, :]

                def step(i, carry):
                    spot = (i // 4, block(lax.rem(i, 4), 32), slice(None))
                    final[spot] = (mine[spot].astype(F32) + got[spot].astype(F32)) + got_two[
                        spot
                    ].astype(F32)
                    return carry

                lax.fori_loop(0, got.shape[0] * 4, step, 0)
        if self.by_rows:
            where = self.total.at[:, :, block(here.c, CHUNK)]
        else:
            where = self.total.at[:, block(here.c, CHUNK), :]
        self.keep = pltpu.make_async_copy(self.final.at[here.c], where, self.local)
        self.keep.start()
        self.give = push(
            self.final.at[1 - here.c],
            where,
            self.last_sem.at[0],
            self.last_sem.at[1],
            here.plane(*PARTNER),
        )

    def sent(self):
        self.keep.wait()
        self.give.wait_send()

    def finish(self):
        for copy in self.first:
            copy.wait_send()
        for copy in self.second:
            copy.wait_send()
        self.give.wait_recv()


def scatter_scratch(width):
    return [
        pltpu.VMEM((8, width, HALF, CHUNK), BF16),
        pltpu.VMEM((4, width, HALF, CHUNK), BF16),
        pltpu.SemaphoreType.DMA((2, 8)),
        pltpu.SemaphoreType.DMA((2, 4)),
        pltpu.SemaphoreType.DMA((2,)),
        pltpu.SemaphoreType.DMA,
    ]


SCATTER = 6


class TensorSum:
    def __init__(self, here, part, bufs):
        self.here, self.part = here, part
        self.pair, self.out, self.inn, self.pair_sem, self.sem = bufs

    def start(self):
        here = self.here
        self.swap = push(
            self.part.at[1 - here.c],
            self.pair,
            self.pair_sem.at[0],
            self.pair_sem.at[1],
            here.plane(*PARTNER),
        )

    def spread(self):
        here = self.here
        self.swap.wait_recv()
        self.sent = []
        for step in (2, 1, 3):
            rows = block(lax.rem(here.z + step, 4), ROWS)
            self.out[step - 1] = (
                self.part[here.c, rows, :].astype(F32) + self.pair[rows, :].astype(F32)
            ).astype(self.out.dtype)
            self.sent.append(
                push(
                    self.out.at[step - 1],
                    self.inn.at[step - 1],
                    self.sem.at[0, step - 1],
                    self.sem.at[1, step - 1],
                    here.along(step),
                )
            )

    def result(self):
        here = self.here
        rows = block(here.z, ROWS)
        total = self.part[here.c, rows, :].astype(F32) + self.pair[rows, :].astype(F32)
        for copy in self.sent:
            copy.wait_recv()
        for step in (1, 2, 3):
            total = total + self.inn[step - 1].astype(F32)
        return total

    def finish(self):
        self.swap.wait_send()
        for copy in self.sent:
            copy.wait_send()


def sum_scratch(length, width):
    return [
        pltpu.VMEM((length, width), BF16),
        pltpu.VMEM((3, ROWS, width), BF16),
        pltpu.VMEM((3, ROWS, width), BF16),
        pltpu.SemaphoreType.DMA((2,)),
        pltpu.SemaphoreType.DMA((2, 3)),
    ]


class TensorGather:
    def __init__(self, here, mine, whole, sem, pair_sem, local):
        self.here, self.mine, self.whole = here, mine, whole
        self.sem, self.pair_sem, self.local = sem, pair_sem, local

    def start(self):
        here = self.here
        place = self.whole.at[here.c, block(here.z, ROWS), :]
        self.sent = []
        for step in (2, 1, 3):
            self.sent.append(
                push(
                    self.mine,
                    place,
                    self.sem.at[0, step - 1],
                    self.sem.at[1, step - 1],
                    here.along(step),
                )
            )
        self.shared = [
            push(
                self.mine,
                place,
                self.pair_sem.at[0, 0],
                self.pair_sem.at[1, 0],
                here.plane(*PARTNER),
            )
        ]
        self.own = pltpu.make_async_copy(self.mine, place, self.local)
        self.own.start()

    def forward(self):
        here = self.here
        for index, step in enumerate((2, 1, 3)):
            self.sent[index].wait_recv()
            place = self.whole.at[here.c, block(here.behind(step), ROWS), :]
            self.shared.append(
                push(
                    place,
                    place,
                    self.pair_sem.at[0, step],
                    self.pair_sem.at[1, step],
                    here.plane(*PARTNER),
                )
            )

    def finish(self):
        for copy in self.sent:
            copy.wait_send()
        for copy in self.shared:
            copy.wait()
        self.own.wait()


class LineSum:
    def __init__(self, here, part, bufs):
        self.here, self.part = here, part
        self.pair, self.slot, self.pair_sem, self.sem = bufs

    def start(self):
        here = self.here
        self.swap = push(
            self.part.at[1 - here.c],
            self.pair,
            self.pair_sem.at[0],
            self.pair_sem.at[1],
            here.plane(*PARTNER),
        )

    def own(self, z):
        rows = block(z, ROWS)
        return self.part[self.here.c, rows, :].astype(F32) + self.pair[rows, :].astype(F32)

    def depth(self, way):
        return self.here.z if way == 0 else 3 - self.here.z

    def hop(self, way, k, src):
        here = self.here
        return pltpu.make_async_remote_copy(
            src_ref=src,
            dst_ref=self.slot.at[way, k],
            send_sem=self.sem.at[0, way, k],
            recv_sem=self.sem.at[1, way, k],
            device_id=(here.x * 2 + here.c, here.y, here.z + (1 if way == 0 else -1)),
            device_id_type=MESH,
        )

    def take(self, way, k):
        here = self.here
        pltpu.make_async_remote_copy(
            src_ref=self.slot.at[way, k],
            dst_ref=self.slot.at[way, k],
            send_sem=self.sem.at[0, way, k],
            recv_sem=self.sem.at[1, way, k],
            device_id=(here.x * 2 + here.c, here.y, here.z - (1 if way == 0 else -1)),
            device_id_type=MESH,
        ).wait_recv()

    def stage(self, k):
        here = self.here
        if k == 0:
            self.swap.wait_recv()
        for way in (0, 1):
            depth = self.depth(way)
            shard = here.z + 3 - k if way == 0 else here.z - 3 + k

            @pl.when(depth == 0)
            def _():
                self.slot[way, k] = self.own(shard).astype(BF16)
                self.hop(way, k, self.slot.at[way, k]).start()

            if k > 0:

                @pl.when((depth >= 1) & (depth <= k))
                def _():
                    self.take(way, k - 1)
                    self.slot[way, k - 1] = (
                        self.own(shard) + self.slot[way, k - 1].astype(F32)
                    ).astype(BF16)
                    self.hop(way, k, self.slot.at[way, k - 1]).start()

    def result(self):
        total = self.own(self.here.z)
        for way in (0, 1):
            depth = self.depth(way)

            @pl.when(depth >= 1)
            def _():
                self.take(way, 2)

            total = total + jnp.where(depth >= 1, self.slot[way, 2].astype(F32), 0.0)
        return total

    def finish(self):
        self.swap.wait_send()
        for way in (0, 1):
            for k in range(3):

                @pl.when(self.depth(way) <= k)
                def _():
                    self.hop(way, k, self.slot.at[way, k]).wait_send()


def line_scratch(length, width):
    return [
        pltpu.VMEM((length, width), BF16),
        pltpu.VMEM((2, 3, ROWS, width), BF16),
        pltpu.SemaphoreType.DMA((2,)),
        pltpu.SemaphoreType.DMA((2, 2, 3)),
    ]


class LineGather:
    def __init__(self, here, place, sem):
        self.here, self.place, self.sem = here, place, sem

    def hop(self, way, k):
        here = self.here
        step = 1 if way == 0 else -1
        spot = self.place(here.z - k * step)
        return pltpu.make_async_remote_copy(
            src_ref=spot,
            dst_ref=spot,
            send_sem=self.sem.at[0, way, k],
            recv_sem=self.sem.at[1, way, k],
            device_id=(here.x * 2 + here.c, here.y, here.z + step),
            device_id_type=MESH,
        )

    def arrival(self, way, k):
        here = self.here
        step = 1 if way == 0 else -1
        spot = self.place(here.z - (k + 1) * step)
        return pltpu.make_async_remote_copy(
            src_ref=spot,
            dst_ref=spot,
            send_sem=self.sem.at[0, way, k],
            recv_sem=self.sem.at[1, way, k],
            device_id=(here.x * 2 + here.c, here.y, here.z - step),
            device_id_type=MESH,
        )

    def sends(self, way, k):
        z = self.here.z
        return (z >= k) & (z < 3) if way == 0 else (z <= 3 - k) & (z > 0)

    def gets(self, way, k):
        z = self.here.z
        return z >= k + 1 if way == 0 else z <= 2 - k

    def start(self):
        for way in (0, 1):

            @pl.when(self.sends(way, 0))
            def _():
                self.hop(way, 0).start()

    def onward(self, k, then=None):
        for way in (0, 1):

            @pl.when(self.gets(way, k))
            def _():
                self.arrival(way, k).wait_recv()
                if then is not None:
                    then(self.here.z - (k + 1) * (1 if way == 0 else -1))

            if k < 2:

                @pl.when(self.sends(way, k + 1))
                def _():
                    self.hop(way, k + 1).start()

    def finish(self):
        for way in (0, 1):
            for k in range(3):

                @pl.when(self.sends(way, k))
                def _():
                    self.hop(way, k).wait_send()


def normed(values):
    center = values - jnp.mean(values, -1, keepdims=True)
    variance = jnp.mean(center * center, -1, keepdims=True)
    inv_std = lax.rsqrt(variance + NORM_EPS)
    return (center * inv_std, inv_std)


def norm_row(packs, row):
    return jnp.concatenate([packs[k, row : row + 1, :] for k in range(8)], 1)


def params(ident, limit=60):
    return pltpu.CompilerParams(
        collective_id=ident, has_side_effects=True, vmem_limit_bytes=limit << 20
    )


def cast_rows(raw, shard):
    count, rows, _ = raw.shape
    for j in range(count):

        def step(i, carry):
            at = pl.ds(pl.multiple_of(i * 32, 32), 32)
            shard[j, at, :] = raw[j, at, :].astype(BF16)
            return carry

        lax.fori_loop(0, rows // 32, step, 0)


def front_kernel(*refs):
    head_count, position, bucket, tok, cot, norm_master = refs[:6]
    masters = refs[6:10]
    n1, both_cot, tables, packs, n2, mid, q_out, k_out, v_out, a_out = refs[10:20]
    wholes = refs[20:24]
    raws, shards = refs[24:28], refs[28:32]
    raw_sem, n2_own, part, small, pair, local = refs[32:38]
    sums, tensor_sems, gather_refs = refs[38:43], refs[43:46], refs[46:58]
    here = Here()
    loads = []
    for i in range(4):
        loads.append(pltpu.make_async_copy(masters[i], raws[i], raw_sem.at[i]))
        loads[i].start()
    me = here.chunk(0, 0, 0)
    lane = lax.broadcasted_iota(jnp.int32, (1, CHUNK), 1)
    counts = jnp.zeros((1, CHUNK), F32)
    for c in range(4):
        count = jnp.sum((bucket[...] == c).astype(F32), 1, keepdims=True)
        counts = counts + jnp.where(lane == c, count, 0.0)
    packs[pl.ds(me, 1)] = jnp.concatenate(
        [norm_master[...].astype(BF16).astype(F32), counts, jnp.zeros((3, CHUNK), F32)], 0
    )[None]
    gathers = [
        Gather(here, i in (0, 2), shards[i], wholes[i], *gather_refs[i * 3 : i * 3 + 3])
        for i in range(4)
    ]
    loads[0].wait()
    cast_rows(raws[0], shards[0])
    greet(here, PLANE, (1, 2, 3))
    gathers[0].start()
    packed = []
    for index, peer in enumerate(PLANE):
        packed.append(
            push(
                packs.at[me], packs.at[me],
                small.at[0, index], small.at[1, index], here.plane(*peer),
            )
        )
    partner = here.plane(*PARTNER)
    table = tables.at[here.c]
    fill_table(table, position[...], bucket[...], head_count[0])
    shared = [
        push(table, table, pair.at[0, 0], pair.at[1, 0], partner),
        push(cot, both_cot.at[here.c], pair.at[0, 1], pair.at[1, 1], partner),
    ]
    keep = pltpu.make_async_copy(cot, both_cot.at[here.c], local)
    keep.start()
    for i in range(1, 4):
        loads[i].wait()
        cast_rows(raws[i], shards[i])
    for copy in packed:
        copy.wait()
    gain, shift = norm_row(packs, 0), norm_row(packs, 1)
    mine = n1.at[here.c]

    def rows_step(i, carry):
        rows = block(i, 32)
        hat, _ = normed(tok[rows, :].astype(F32))
        mine[rows, :] = (hat * gain + shift).astype(BF16)
        return carry

    lax.fori_loop(0, tok.shape[0] // 32, rows_step, 0)
    shared.append(push(mine, mine, pair.at[0, 2], pair.at[1, 2], partner))
    gathers[1].start()
    gathers[0].forward()
    gathers[1].forward()
    gathers[0].finish()
    gathers[2].start()
    gathers[3].start()
    shared[0].wait_recv()
    shared[2].wait_recv()
    head0 = here.z * 4 + here.c * 2
    attend_body(head0, n1, wholes[0], wholes[1], tables, q_out, k_out, v_out, a_out, part)
    gathers[1].finish()
    total = TensorSum(here, part, sums)
    attend_out(a_out, wholes[1], part, 1 - here.c)
    total.start()
    attend_out(a_out, wholes[1], part, here.c)
    total.spread()
    rows = block(here.z, ROWS)
    middle = tok[rows, :].astype(F32) + total.result()
    mid[...] = middle
    hat, _ = normed(middle)
    n2_own[...] = (hat * norm_row(packs, 2) + norm_row(packs, 3)).astype(BF16)
    gather = TensorGather(here, n2_own, n2, *tensor_sems)
    gather.start()
    gathers[2].forward()
    gathers[3].forward()
    gather.forward()
    total.finish()
    gather.finish()
    gathers[2].finish()
    gathers[3].finish()
    keep.wait()
    shared[0].wait_send()
    shared[1].wait()
    shared[2].wait_send()


def front_call(head_count, position, bucket, tok, cot, norm_master, masters):
    length, width = tok.shape
    both = jax.ShapeDtypeStruct((2, length, width), BF16)
    thin = jax.ShapeDtypeStruct((2 * length, CHUNK), BF16)
    wholes = [
        jax.ShapeDtypeStruct((3, width, CHUNK), BF16),
        jax.ShapeDtypeStruct((1, CHUNK, width), BF16),
        jax.ShapeDtypeStruct((4, width, CHUNK), BF16),
        jax.ShapeDtypeStruct((4, CHUNK, width), BF16),
    ]
    results = pl.pallas_call(
        front_kernel,
        out_shape=[
            both,
            both,
            jax.ShapeDtypeStruct((2, 5, length, HALF), F32),
            jax.ShapeDtypeStruct((8, 8, CHUNK), F32),
            both,
            jax.ShapeDtypeStruct((ROWS, width), F32),
            thin, thin, thin, thin,
        ]
        + wholes,
        in_specs=[SM, VM, VM, VM, VM, VM] + [ANY] * 4,
        out_specs=[VM, ANY, VM, VM, ANY, VM, VM, VM, VM, VM, VM, VM, ANY, ANY],
        scratch_shapes=[pltpu.VMEM(master.shape, F32) for master in masters]
        + [pltpu.VMEM(master.shape, BF16) for master in masters]
        + [
            pltpu.SemaphoreType.DMA((4,)),
            pltpu.VMEM((ROWS, width), BF16),
            pltpu.VMEM((2, length, width), BF16),
            pltpu.SemaphoreType.DMA((2, 7)),
            pltpu.SemaphoreType.DMA((2, 3)),
            pltpu.SemaphoreType.DMA,
        ]
        + sum_scratch(length, width)
        + tensor_gather_sems()
        + gather_sems() * 4,
        compiler_params=params(1),
        name="front",
    )(head_count, position, bucket, tok, cot, norm_master, *masters)
    return results[:10], results[10:]


def tensor_gather_sems():
    return [
        pltpu.SemaphoreType.DMA((2, 3)),
        pltpu.SemaphoreType.DMA((2, 4)),
        pltpu.SemaphoreType.DMA,
    ]


def norm_back(grad_out, hat, inv_std, gain):
    scaled = grad_out * gain
    inner = (
        scaled
        - jnp.mean(scaled, -1, keepdims=True)
        - hat * jnp.mean(scaled * hat, -1, keepdims=True)
    )
    return (
        inner * inv_std,
        jnp.sum(grad_out * hat, 0, keepdims=True),
        jnp.sum(grad_out, 0, keepdims=True),
    )


def ffn_hidden(r, n2, cot, bucket, wu, wd, squares, grad_hidden):
    width = n2.shape[2]
    hidden = dot(n2[...].reshape(-1, width), wu[r])
    live = bucket >= jnp.float32(r)
    rectified = jnp.maximum(jnp.where(live, hidden, 0.0), 0.0)
    squares[r] = (rectified * rectified).astype(BF16)
    grad_square = dot(cot[...].reshape(-1, width), wd[r], ((1,), (1,)))
    grad_hidden[r] = (grad_square * 2.0 * rectified).astype(BF16)


def ffn_rows(s, left, right, part, transposed):
    length, width = part.shape[1:]
    rows = pl.ds(pl.multiple_of(s * length, length), length)
    for n in range(width // (2 * CHUNK)):
        cols = slice(n * 2 * CHUNK, (n + 1) * 2 * CHUNK)
        total = None
        for r in range(4):
            if transposed:
                term = dot(left[r, rows, :], right[r, cols, :], ((1,), (1,)))
            else:
                term = dot(left[r, rows, :], right[r, :, cols])
            total = term if total is None else total + term
        part[s, :, cols] = total.astype(BF16)


def attend_back_body(head0, gm, qkva, wq, wo, tables, dp, part):
    length = tables.shape[2]
    width = gm.shape[2]
    q_rows, k_rows, v_rows = qkva.at[0], qkva.at[1], qkva.at[2]
    grad_att = dot(gm[...].reshape(2 * length, width), wo[...], ((1,), (1,))).astype(BF16)
    for s in range(2):
        rows = slice(s * length, (s + 1) * length)
        cosine, sine = tables[s, 0], tables[s, 1]
        lowest = tables[s, 2, :, 0:1]
        for h in range(2):
            cols = slice(h * HEAD_DIM, (h + 1) * HEAD_DIM)
            active = tables[s, 4] > (head0 + h).astype(F32)
            grad_heads = jnp.where(active, grad_att[rows, cols].astype(F32), 0.0).astype(BF16)
            queries, key_rows, value_rows = q_rows[rows, cols], k_rows[rows, cols], v_rows[rows, cols]
            weights = attention_weights(queries, key_rows, lowest)
            grad_weights = dot(grad_heads, value_rows, ((1,), (1,)))
            inner = jnp.sum(weights * grad_weights, -1, keepdims=True)
            grad_scores = (weights * (grad_weights - inner)).astype(BF16)
            grad_query = dot(grad_scores, key_rows) * HEAD_DIM ** (-0.5)
            grad_keys = dot(grad_scores, queries, ((0,), (0,)))
            grad_values = dot(weights.astype(BF16), grad_heads, ((0,), (0,)))
            dp[0, rows, cols] = turn(grad_query, cosine, -sine).astype(BF16)
            dp[1, rows, cols] = turn(grad_keys, cosine, -sine).astype(BF16)
            dp[2, rows, cols] = grad_values.astype(BF16)


def attend_back_rows(s, dp, wq, part):
    length = part.shape[1]
    rows = pl.ds(pl.multiple_of(s * length, length), length)
    total = dot(dp[0, rows, :], wq[0], ((1,), (1,)))
    total = total + dot(dp[1, rows, :], wq[1], ((1,), (1,)))
    total = total + dot(dp[2, rows, :], wq[2], ((1,), (1,)))
    part[s] = total.astype(BF16)


def norm_share(here, values, bufs):
    slices, heard, plane_sum, heard_z, ns, nz = bufs
    for k in range(8):
        slices[k, 0:4, :] = values[:, k * CHUNK : (k + 1) * CHUNK]
        slices[k, 4:8, :] = jnp.zeros((4, CHUNK), F32)
    copies = []
    for index, peer in enumerate(PLANE):
        copies.append(
            push(
                slices.at[here.chunk(*peer)],
                heard.at[index],
                ns.at[0, index],
                ns.at[1, index],
                here.plane(*peer),
            )
        )
    return copies


def norm_share_along(here, copies, bufs):
    slices, heard, plane_sum, heard_z, ns, nz = bufs
    mine = slices[here.chunk(0, 0, 0)]
    for index in range(7):
        copies[index].wait()
        mine = mine + heard[index]
    plane_sum[...] = mine
    onward = []
    for step in (1, 2, 3):
        onward.append(
            push(
                plane_sum,
                heard_z.at[here.z],
                nz.at[0, step - 1],
                nz.at[1, step - 1],
                here.along(step),
            )
        )
    heard_z[pl.ds(here.z, 1)] = mine[None]
    return onward


def back_kernel(*refs):
    n2, cot, tables, packs, mid = refs[0:5]
    tok, wq, wo, wu, wd, n1, q_rows, k_rows, v_rows, a_rows = refs[5:15]
    out_all, ig_own, norm_total, q_sum, o_sum, u_sum, d_sum = refs[15:22]
    wu_v, wd_v, qkva, tok_own, load_sem, squares, grad_hidden, part, part_f, dp = refs[22:32]
    gu, gd, gq, go, gm, dmid, sums, out_v = refs[32:40]
    back_bufs, branch_bufs, final_one, final_two = refs[40:44], refs[44:48], refs[48], refs[49]
    gm_sem, gm_pair, out_sem, keep_sem, norm_bufs = *refs[50:54], refs[54:60]
    rest = refs[60:]
    here = Here()
    loads = []

    def load(src, dst):
        copy = pltpu.make_async_copy(src, dst, load_sem.at[len(loads)])
        copy.start()
        loads.append(copy)
        return copy

    first = [(load(wu.at[r], wu_v.at[r]), load(wd.at[r], wd_v.at[r])) for r in range(4)]
    small = [load(src, qkva.at[i]) for i, src in enumerate((q_rows, k_rows, v_rows, a_rows))]
    place = block(here.z, ROWS)
    small.append(load(tok.at[place, :], tok_own))
    scatters = [
        Scatter(here, by_rows, grad, total, rest[i * SCATTER : (i + 1) * SCATTER] + (final,))
        for i, (by_rows, grad, total, final) in enumerate(
            (
                (True, gu.at[0:1], u_sum.at[0:1], final_one.at[:, 0:1]),
                (False, gd.at[0:1], d_sum.at[0:1], final_two.at[:, 0:1]),
                (True, gu.at[1:4], u_sum.at[1:4], final_one.at[:, 1:4]),
                (False, gd.at[1:4], d_sum.at[1:4], final_two.at[:, 1:4]),
                (True, gq, q_sum, final_one.at[:, 0:3]),
                (False, go, o_sum, final_one.at[:, 3:4]),
            )
        )
    ]
    early_u, early_d, scatter_u, scatter_d, scatter_q, scatter_o = scatters
    length, width = n2.shape[1:]

    def up_gradient(r):
        rows_in = n2[...].reshape(2 * length, width)
        gu[r] = dot(rows_in, grad_hidden[r], ((0,), (0,))).astype(BF16)

    def down_gradient(r):
        grads_in = cot[...].reshape(2 * length, width)
        gd[r] = dot(squares[r], grads_in, ((0,), (0,))).astype(BF16)

    bucket = jnp.concatenate([tables[0, 3, :, 0:1], tables[1, 3, :, 0:1]], 0)
    for r in range(4):
        first[r][0].wait()
        first[r][1].wait()
        ffn_hidden(r, n2, cot, bucket, wu_v, wd_v, squares, grad_hidden)
        if r == 0:
            up_gradient(0)
            greet(here, PLANE, (1, 2, 3))
            early_u.start()
            down_gradient(0)
            early_d.start()
    other = 1 - here.c
    back = LineSum(here, part, back_bufs)
    ffn_rows(other, grad_hidden, wu_v, part, True)
    back.start()
    ffn_rows(here.c, grad_hidden, wu_v, part, True)
    back.stage(0)
    load_q = load(wq, wu_v.at[0:3])
    for r in range(1, 4):
        up_gradient(r)
    scatter_u.start()
    down_gradient(1)
    back.stage(1)
    down_gradient(2)
    down_gradient(3)
    scatter_d.start()
    branch = LineSum(here, part_f, branch_bufs)
    ffn_rows(other, squares, wd_v, part_f, False)
    branch.start()
    back.stage(2)
    ffn_rows(here.c, squares, wd_v, part_f, False)
    load_n1 = load(n1, wd_v.at[0:2])
    load_o = load(wo, wd_v.at[2:3])
    grad_n2 = back.result().astype(BF16).astype(F32)
    back.finish()
    hat, inv_std = normed(mid[...])
    grad_mid, gain_sum, shift_sum = norm_back(grad_n2, hat, inv_std, norm_row(packs, 2))
    grad_mid = cot[here.c, place, :].astype(F32) + grad_mid
    dmid[...] = grad_mid
    gm[pl.ds(here.c, 1), place, :] = grad_mid.astype(BF16)[None]
    gather = LineGather(here, lambda z: gm.at[here.c, block(z, ROWS), :], gm_sem)
    gather.start()
    early_u.middle()
    early_d.middle()

    def shared(z):
        spot = gm.at[here.c, block(z, ROWS), :]
        return pltpu.make_async_remote_copy(
            src_ref=spot,
            dst_ref=spot,
            send_sem=gm_pair.at[0, z],
            recv_sem=gm_pair.at[1, z],
            device_id=here.plane(*PARTNER),
            device_id_type=MESH,
        )

    shared(here.z).start()
    sums[0:1, :] = gain_sum
    sums[1:2, :] = shift_sum
    gather.onward(0, lambda z: shared(z).start())
    branch.stage(0)
    gather.onward(1, lambda z: shared(z).start())
    gather.onward(2, lambda z: shared(z).start())
    branch.stage(1)
    scatter_u.middle()
    for copy in small:
        copy.wait()
    load_o.wait()
    load_q.wait()
    load_n1.wait()
    gather.finish()
    for z in range(4):
        shared(z).wait()
    head0 = here.z * 4 + here.c * 2
    attend_back_body(head0, gm, qkva, wu_v, wd_v.at[2], tables, dp, part)
    branch.stage(2)
    last = LineSum(here, part, back_bufs)
    attend_back_rows(other, dp, wu_v, part)
    last.start()
    attend_back_rows(here.c, dp, wu_v, part)
    last.stage(0)
    scatter_d.middle()
    rows_in = wd_v[0:2].reshape(2 * length, width)
    for j in range(3):
        gq[j] = dot(rows_in, dp[j], ((0,), (0,))).astype(BF16)
    scatter_q.start()
    last.stage(1)
    go[0] = dot(qkva[3], gm[...].reshape(2 * length, width), ((0,), (0,))).astype(BF16)
    scatter_o.start()
    early_u.last()
    early_d.last()
    last.stage(2)
    out_v[place, :] = (mid[...] + branch.result().astype(BF16).astype(F32)).astype(BF16)
    spread = LineGather(here, lambda z: out_v.at[block(z, ROWS), :], out_sem)
    spread.start()
    scatter_u.last()
    spread.onward(0)
    grad_n1 = last.result()
    hat, inv_std = normed(tok_own[...].astype(F32))
    grad_in, gain_sum, shift_sum = norm_back(grad_n1, hat, inv_std, norm_row(packs, 0))
    ig_own[...] = (dmid[...] + grad_in).astype(BF16)
    norm_copies = norm_share(
        here, jnp.concatenate([gain_sum, shift_sum, sums[...]], 0), norm_bufs
    )
    scatter_q.middle()
    scatter_o.middle()
    spread.onward(1)
    spread.onward(2)
    keep = pltpu.make_async_copy(out_v, out_all, keep_sem)
    keep.start()
    onward = norm_share_along(here, norm_copies, norm_bufs)
    scatter_d.last()
    for copy in onward:
        copy.wait()
    heard_z = norm_bufs[3]
    norm_total[...] = ((heard_z[0] + heard_z[1]) + heard_z[2]) + heard_z[3]
    early_u.sent()
    scatter_u.sent()
    scatter_q.last()
    scatter_o.last()
    branch.finish()
    last.finish()
    spread.finish()
    keep.wait()
    for scatter in (early_d, scatter_d, scatter_q, scatter_o):
        scatter.sent()
    for scatter in scatters:
        scatter.finish()


def back_call(n2, cot, tables, packs, mid, tok, wq, wo, wu, wd, n1, rows):
    _, length, width = n2.shape
    both = pltpu.VMEM((2, length, width), BF16)
    results = pl.pallas_call(
        back_kernel,
        out_shape=[
            jax.ShapeDtypeStruct((length, width), BF16),
            jax.ShapeDtypeStruct((ROWS, width), BF16),
            jax.ShapeDtypeStruct((8, CHUNK), F32),
            jax.ShapeDtypeStruct((3, CHUNK, 2 * CHUNK), F32),
            jax.ShapeDtypeStruct((1, 2 * CHUNK, CHUNK), F32),
            jax.ShapeDtypeStruct((4, CHUNK, 2 * CHUNK), F32),
            jax.ShapeDtypeStruct((4, 2 * CHUNK, CHUNK), F32),
        ],
        in_specs=[VM] * 5 + [ANY] * 10,
        out_specs=[ANY, VM, VM, ANY, ANY, ANY, ANY],
        scratch_shapes=[
            pltpu.VMEM(wu.shape, BF16),
            pltpu.VMEM(wd.shape, BF16),
            pltpu.VMEM((4, 2 * length, CHUNK), BF16),
            pltpu.VMEM((ROWS, width), BF16),
            pltpu.SemaphoreType.DMA((16,)),
            pltpu.VMEM((4, 2 * length, CHUNK), BF16),
            pltpu.VMEM((4, 2 * length, CHUNK), BF16),
            both,
            both,
            pltpu.VMEM((3, 2 * length, CHUNK), BF16),
            pltpu.VMEM(wu.shape, BF16),
            pltpu.VMEM(wd.shape, BF16),
            pltpu.VMEM(wq.shape, BF16),
            pltpu.VMEM(wo.shape, BF16),
            both,
            pltpu.VMEM((ROWS, width), F32),
            pltpu.VMEM((2, width), F32),
            pltpu.VMEM((length, width), BF16),
        ]
        + line_scratch(length, width) * 2
        + [pltpu.VMEM((2, 4, CHUNK, CHUNK), F32)] * 2
        + [
            pltpu.SemaphoreType.DMA((2, 2, 3)),
            pltpu.SemaphoreType.DMA((2, 4)),
            pltpu.SemaphoreType.DMA((2, 2, 3)),
            pltpu.SemaphoreType.DMA,
            pltpu.VMEM((8, 8, CHUNK), F32),
            pltpu.VMEM((7, 8, CHUNK), F32),
            pltpu.VMEM((8, CHUNK), F32),
            pltpu.VMEM((4, 8, CHUNK), F32),
            pltpu.SemaphoreType.DMA((2, 7)),
            pltpu.SemaphoreType.DMA((2, 3)),
        ]
        + (scatter_scratch(1) * 2 + scatter_scratch(3) * 2)
        + scatter_scratch(3)
        + scatter_scratch(1),
        compiler_params=params(3),
        name="back",
    )(n2, cot, tables, packs, mid, tok, wq, wo, wu, wd, n1, *rows)
    return results


FIRST_SCALE = 1.0 / (1.0 - BETA_FIRST**STEP)
SECOND_SCALE = 1.0 / (1.0 - BETA_SECOND**STEP)


def folded(values):
    rows, cols = values.shape
    total = None
    for i in range(rows // 8):
        for j in range(cols // 128):
            tile = values[i * 8 : i * 8 + 8, j * 128 : j * 128 + 128]
            total = tile if total is None else total + tile
    return total


def updated(weight, gradient, first_old, second_old):
    first_new = BETA_FIRST * first_old + (1.0 - BETA_FIRST) * gradient
    second_new = BETA_SECOND * second_old + (1.0 - BETA_SECOND) * gradient * gradient
    update = first_new * FIRST_SCALE / (
        jnp.sqrt(second_new * SECOND_SCALE) + ADAM_EPS
    ) + WEIGHT_DECAY * weight
    return (update, first_new, second_new)


AHEAD = 4


def adam_kernel(*refs):
    sources = [refs[kind * 5 : kind * 5 + 4] for kind in range(4)]
    norm_grad, norm_master, norm_first, norm_second = [refs[kind * 5 + 4] for kind in range(4)]
    out_all = refs[20]
    outs = [refs[21 + kind * 5 : 25 + kind * 5] for kind in range(3)]
    norm_outs = [refs[25 + kind * 5] for kind in range(3)]
    tile, output = refs[36:38]
    held = [refs[38 + kind * 4 : 42 + kind * 4] for kind in range(4)]
    load_sem, store_sem = refs[54:56]
    blocks = [(i, j) for i in range(4) for j in range(sources[0][i].shape[0])]
    bases = [sum(source.shape[0] for source in sources[0][:i]) for i in range(4)]

    def loading(kind, i, j):
        return pltpu.make_async_copy(
            sources[kind][i].at[j], held[kind][i].at[j], load_sem.at[kind, bases[i] + j]
        )

    def storing(kind, i, j):
        return pltpu.make_async_copy(
            held[(0, 2, 3)[kind]][i].at[j], outs[kind][i].at[j], store_sem.at[kind, bases[i] + j]
        )

    for i, j in blocks:
        for kind in range(4):
            loading(kind, i, j).start()
    output[...] = out_all[...].astype(F32)
    weight = norm_master[...]
    update, first_new, second_new = updated(
        weight, norm_grad[0:4, :], norm_first[...], norm_second[...]
    )
    for out, value in zip(norm_outs, (update, first_new, second_new)):
        out[...] = value
    for row, value in ((4, weight), (12, update)):
        square = value * value * 0.25
        tile[row : row + 4, :] = square[:, :128] + square[:, 128:]
    for i in range(4):
        grads, masters, firsts, seconds = [held[kind][i] for kind in range(4)]

        def one_block(j, sums):
            for kind in range(4):
                loading(kind, i, j).wait()

            def step(k, carry):
                at = pl.ds(pl.multiple_of(k * 32, 32), 32)
                weight = masters[j, at, :]
                update, first_new, second_new = updated(
                    weight, grads[j, at, :], firsts[j, at, :], seconds[j, at, :]
                )
                grads[j, at, :] = update
                firsts[j, at, :] = first_new
                seconds[j, at, :] = second_new
                return (carry[0] + folded(weight * weight), carry[1] + folded(update * update))

            sums = lax.fori_loop(0, grads.shape[1] // 32, step, sums)
            for kind in range(3):
                storing(kind, i, j).start()
            return sums

        zero = jnp.zeros((8, 128), F32)
        sums = lax.fori_loop(0, grads.shape[0], one_block, (zero, zero))
        tile[i : i + 1, :] = jnp.sum(sums[0], 0, keepdims=True)
        tile[8 + i : 9 + i, :] = jnp.sum(sums[1], 0, keepdims=True)
    for i, j in blocks:
        for kind in range(3):
            storing(kind, i, j).wait()


def adam_call(grads, masters, firsts, seconds, out_all):
    shapes = [master.shape for master in masters]
    like = [jax.ShapeDtypeStruct(shape, F32) for shape in shapes]
    specs = [ANY] * 4 + [VM]
    count = sum(shape[0] for shape in shapes[:4])
    results = pl.pallas_call(
        adam_kernel,
        out_shape=like * 3
        + [jax.ShapeDtypeStruct((16, 128), F32), jax.ShapeDtypeStruct(out_all.shape, F32)],
        in_specs=specs * 4 + [VM],
        out_specs=specs * 3 + [VM, VM],
        scratch_shapes=[pltpu.VMEM(shape, F32) for shape in shapes[:4]] * 4
        + [pltpu.SemaphoreType.DMA((4, count)), pltpu.SemaphoreType.DMA((3, count))],
        compiler_params=local_params(60),
        name="adam",
    )(*grads, *masters, *firsts, *seconds, out_all)
    return results[0:5], results[5:10], results[10:15], results[15], results[16]


def total_kernel(tile, norms, tiles_z, plane_tile, tiles, zs, ps):
    here = Here()
    greet(here, PLANE, (1, 2, 3))
    sent = []
    for step in (2, 1, 3):
        sent.append(
            push(tile, tiles_z.at[here.z], zs.at[0, step - 1], zs.at[1, step - 1], here.along(step))
        )
    tiles_z[pl.ds(here.z, 1)] = tile[...][None]
    for copy in sent:
        copy.wait()
    plane_tile[...] = ((tiles_z[0] + tiles_z[1]) + tiles_z[2]) + tiles_z[3]
    me = here.chunk(0, 0, 0)
    sent = []
    for index, peer in enumerate(PLANE):
        sent.append(
            push(plane_tile, tiles.at[me], ps.at[0, index], ps.at[1, index], here.plane(*peer))
        )
    tiles[pl.ds(me, 1)] = plane_tile[...][None]
    for copy in sent:
        copy.wait()
    total = tiles[0]
    for k in range(1, 8):
        total = total + tiles[k]
    roots = jnp.sqrt(jnp.sum(total, 1, keepdims=True))
    norms[...] = jnp.broadcast_to(roots, norms.shape)


def total_call(tile):
    return pl.pallas_call(
        total_kernel,
        out_shape=jax.ShapeDtypeStruct((16, 128), F32),
        in_specs=[VM],
        out_specs=VM,
        scratch_shapes=[
            pltpu.VMEM((4, 16, 128), F32),
            pltpu.VMEM((16, 128), F32),
            pltpu.VMEM((8, 16, 128), F32),
            pltpu.SemaphoreType.DMA((2, 3)),
            pltpu.SemaphoreType.DMA((2, 7)),
        ],
        compiler_params=params(5),
        name="norm_totals",
    )(tile)


def weight_kernel(*refs):
    norms, updates, masters, packs = refs[0], refs[1:6], refs[6:11], refs[11]
    ig_rows = refs[12:16]
    outs = refs[16:21]
    igrad, lamb_norms, share = refs[21:24]
    held = (refs[24:28], refs[28:32])
    load_sem, store_sem = refs[32:34]
    blocks = [(i, j) for i in range(4) for j in range(updates[i].shape[0])]
    loads = []

    def load():
        index = len(loads)
        if index == len(blocks):
            return
        i, j = blocks[index]
        loads.append([])
        for kind, source in enumerate((updates, masters)):
            copy = pltpu.make_async_copy(
                source[i].at[j], held[kind][i].at[j], load_sem.at[kind, index]
            )
            copy.start()
            loads[index].append(copy)

    for _ in range(AHEAD):
        load()
    scales = LEARN_RATE * (norms[0:8, 0:1] / norms[8:16, 0:1])
    outs[4][...] = masters[4][...] - scales[4:8, :] * updates[4][...]
    row = lax.broadcasted_iota(jnp.int32, norms.shape, 0)
    lane = lax.broadcasted_iota(jnp.int32, norms.shape, 1)
    flat = jnp.sum(jnp.where(row == lane, norms[...], 0.0), 0, keepdims=True)
    lamb_norms[0:1, :] = flat[:, 0:8]
    lamb_norms[1:2, :] = flat[:, 8:16]
    counts = packs[0, 4:5, :]
    for k in range(1, 8):
        counts = counts + packs[k, 4:5, :]
    share[...] = counts[:, 0:4] / (igrad.shape[0] * 8)
    here = Here()
    for step in range(4):
        igrad[block(here.behind(step), ROWS), :] = ig_rows[step][...].astype(F32)
    stores = []
    for index, (i, j) in enumerate(blocks):
        for copy in loads[index]:
            copy.wait()
        load()
        scale = scales[i : i + 1, :]

        def step(k, carry):
            at = pl.ds(pl.multiple_of(k * 32, 32), 32)
            held[1][i][j, at, :] = held[1][i][j, at, :] - scale * held[0][i][j, at, :]
            return carry

        lax.fori_loop(0, held[1][i].shape[1] // 32, step, 0)
        copy = pltpu.make_async_copy(held[1][i].at[j], outs[i].at[j], store_sem.at[index])
        copy.start()
        stores.append(copy)
    for copy in stores:
        copy.wait()


def weight_call(norms, updates, masters, packs, ig_rows):
    shapes = [master.shape for master in masters]
    specs = [ANY] * 4 + [VM]
    count = sum(shape[0] for shape in shapes[:4])
    rows, width = ig_rows[0].shape
    return pl.pallas_call(
        weight_kernel,
        out_shape=[jax.ShapeDtypeStruct(shape, F32) for shape in shapes]
        + [
            jax.ShapeDtypeStruct((4 * rows, width), F32),
            jax.ShapeDtypeStruct((2, 8), F32),
            jax.ShapeDtypeStruct((1, 4), F32),
        ],
        in_specs=[VM] + specs * 2 + [VM] * 5,
        out_specs=specs + [VM, VM, VM],
        scratch_shapes=[pltpu.VMEM(shape, F32) for shape in shapes[:4]] * 2
        + [pltpu.SemaphoreType.DMA((2, count)), pltpu.SemaphoreType.DMA((count,))],
        compiler_params=local_params(60),
        name="new_weights",
    )(norms, *updates, *masters, packs, *ig_rows)


def turn(values, cosine, sine):
    return values * cosine + pltpu.roll(values, HEAD_DIM // 2, 1) * sine


def dot(left, right, dims=((1,), (0,))):
    return lax.dot_general(left, right, (dims, ((), ())), preferred_element_type=F32)


def attention_weights(queries, key_rows, lowest):
    scores = dot(queries, key_rows, ((1,), (1,)))
    row = lax.broadcasted_iota(jnp.int32, scores.shape, 0)
    col = lax.broadcasted_iota(jnp.int32, scores.shape, 1)
    allowed = (col <= row) & (col.astype(F32) >= lowest)
    scores = jnp.where(allowed, scores, MASKED)
    exp_scores = jnp.exp(scores - jnp.max(scores, -1, keepdims=True))
    return exp_scores / jnp.sum(exp_scores, -1, keepdims=True)


def attend_body(head0, n1, wq, wo, tables, q_out, k_out, v_out, a_out, part):
    length = tables.shape[2]
    rows_in = n1[...].reshape(2 * length, n1.shape[2])
    projected = [dot(rows_in, wq[j]) for j in range(3)]
    for s in range(2):
        rows = slice(s * length, (s + 1) * length)
        cosine, sine = tables[s, 0], tables[s, 1]
        lowest = tables[s, 2, :, 0:1]
        for h in range(2):
            cols = slice(h * HEAD_DIM, (h + 1) * HEAD_DIM)
            queries = (turn(projected[0][rows, cols], cosine, sine) * HEAD_DIM ** (-0.5)).astype(BF16)
            key_rows = turn(projected[1][rows, cols], cosine, sine).astype(BF16)
            value_rows = projected[2][rows, cols].astype(BF16)
            weights = attention_weights(queries, key_rows, lowest).astype(BF16)
            heads = dot(weights, value_rows)
            active = tables[s, 4] > (head0 + h).astype(F32)
            q_out[rows, cols] = queries
            k_out[rows, cols] = key_rows
            v_out[rows, cols] = value_rows
            a_out[rows, cols] = jnp.where(active, heads, 0.0).astype(BF16)


def attend_out(a_out, wo, part, s):
    length = part.shape[1]
    part[s] = dot(a_out[pl.ds(pl.multiple_of(s * length, length), length), :], wo[0]).astype(BF16)


def fill_table(table, position, bucket, head_count):
    length = table.shape[1]
    row = lax.broadcasted_iota(jnp.int32, (length, length), 0)
    col = lax.broadcasted_iota(jnp.int32, (length, length), 1)

    def column(values):
        return jnp.sum(jnp.where(row == col, values.astype(F32), 0.0), 1, keepdims=True)

    place = column(position)
    lane = lax.broadcasted_iota(jnp.int32, (length, HALF), 1)
    half = HEAD_DIM // 2
    second = lane >= half
    freq_index = jnp.where(second, lane - half, lane).astype(F32)
    angles = place * jnp.exp(freq_index * (-2.0 * math.log(ROPE_BASE) / HEAD_DIM))
    table[0] = jnp.cos(angles)
    sine = jnp.sin(angles)
    table[1] = jnp.where(second, sine, -sine)
    index = lax.broadcasted_iota(jnp.int32, (length, HALF), 0).astype(F32)
    table[2] = index - place
    table[3] = jnp.broadcast_to(column(bucket), (length, HALF))
    table[4] = jnp.broadcast_to(head_count.astype(F32), (length, HALF))


def local_params(limit):
    return pltpu.CompilerParams(vmem_limit_bytes=limit << 20)


def fast_body(
    tokens, cotangent, head_counts, positions, buckets,
    in_master, out_master, up_master, down_master, norm_master,
    in_first, out_first, up_first, down_first, norm_first,
    in_second, out_second, up_second, down_second, norm_second,
):
    tok, cot = tokens[0], cotangent[0]
    (n1, both_cot, tables, packs, n2, mid, q_rows, k_rows, v_rows, a_rows), (wq, wo, wu, wd) = front_call(
        head_counts, positions, buckets, tok, cot, norm_master,
        (in_master, out_master[None], up_master, down_master),
    )
    out_all, ig_own, norm_sum, in_sum, out_sum, up_sum, down_sum = back_call(
        n2, both_cot, tables, packs, mid, tok, wq, wo, wu, wd, n1,
        (q_rows, k_rows, v_rows, a_rows),
    )
    ig_rows = [ig_own] + [
        lax.ppermute(ig_own, "tensor", [(i, (i + step) % 4) for i in range(4)])
        for step in (1, 2, 3)
    ]
    masters = (in_master, out_master[None], up_master, down_master, norm_master)
    firsts = (in_first, out_first[None], up_first, down_first, norm_first)
    seconds = (in_second, out_second[None], up_second, down_second, norm_second)
    updates, moments, squares, tile, output = adam_call(
        (in_sum, out_sum, up_sum, down_sum, norm_sum), masters, firsts, seconds, out_all
    )
    norms = total_call(tile)
    *weights, input_grad, lamb_norms, share = weight_call(
        norms, updates, masters, packs, ig_rows
    )
    flat = lambda group: (group[0], group[1][0], group[2], group[3], group[4])
    return (
        output[None],
        input_grad[None],
        share[0],
        lamb_norms,
        *flat(weights),
        *flat(moments),
        *flat(squares),
    )


def solution(mesh):
    placed = (
        P(("dp", "expert"), None, None),
        P(("dp", "expert"), None, None),
        P(("dp", "expert")),
        P(("dp", "expert"), None),
        P(("dp", "expert"), None),
        P(None, ("dp", "expert"), "tensor"),
        P("tensor", ("dp", "expert")),
        P(None, ("dp", "expert"), "tensor"),
        P(None, "tensor", ("dp", "expert")),
        P(None, ("dp", "expert")),
        P(None, ("dp", "expert"), "tensor"),
        P("tensor", ("dp", "expert")),
        P(None, ("dp", "expert"), "tensor"),
        P(None, "tensor", ("dp", "expert")),
        P(None, ("dp", "expert")),
        P(None, ("dp", "expert"), "tensor"),
        P("tensor", ("dp", "expert")),
        P(None, ("dp", "expert"), "tensor"),
        P(None, "tensor", ("dp", "expert")),
        P(None, ("dp", "expert")),
    )
    shape = dict(mesh.shape)
    fits = shape == {"dp": 4, "expert": 2, "tensor": 4}
    return jax.shard_map(
        fast_body if fits else body,
        mesh=mesh,
        in_specs=placed,
        out_specs=(
            P(("dp", "expert"), None, None),
            P(("dp", "expert"), None, None),
            P(),
            P(),
            P(None, ("dp", "expert"), "tensor"),
            P("tensor", ("dp", "expert")),
            P(None, ("dp", "expert"), "tensor"),
            P(None, "tensor", ("dp", "expert")),
            P(None, ("dp", "expert")),
            P(None, ("dp", "expert"), "tensor"),
            P("tensor", ("dp", "expert")),
            P(None, ("dp", "expert"), "tensor"),
            P(None, "tensor", ("dp", "expert")),
            P(None, ("dp", "expert")),
            P(None, ("dp", "expert"), "tensor"),
            P("tensor", ("dp", "expert")),
            P(None, ("dp", "expert"), "tensor"),
            P(None, "tensor", ("dp", "expert")),
            P(None, ("dp", "expert")),
        ),
        check_vma=False,
    )
```

profile of v0, /device:TPU:0, one launch (start us, length us, event | category | flops | bytes accessed | tf_op | source)
XLA Modules:
  0.0 287.7 jit_solution(14169124958047921078)
XLA Ops:
  1.3 121.1 %front.1 = (bf16[2,256,2048]{2,1,0:T(8,128)(2,1)}, bf16[2,256,2048]{2,1,0:T(8,128)(2,1)}, f32[2,5,256,128]{3,2,1,0:T(8,128)}, f32[8,8,256]{2,1,0:T(8,128)}, bf16...) custom-call(s32[1]{0:T(128)S(6)} %copy.39.refs_0_, ...), custom_call_target="tpu_custom_call" | custom-call | tf_op jit(solution)/shard_map/front/pallas_call | solution.py:1148
  122.4 120.8 %back.1 = (bf16[256,2048]{1,0:T(8,128)(2,1)}, bf16[64,2048]{1,0:T(8,128)(2,1)}, f32[8,256]{1,0:T(8,128)}, f32[3,256,512]{2,1,0:T(8,128)}, f32[1,512,256]{2,1,0:T...) custom-call(bf16[2,256,2048]{2,1,0:T(8,128)(2,1)} %get-tuple-element.65.refs_0_, ...), custom_call_target="tpu_custom_call" | custom-call | tf_op jit(solution)/shard_map/back/pallas_call | solution.py:1483
  243.2 2.1 collective-permute-start.2
  245.3 0.2 collective-permute-start.1
  245.5 0.8 collective-permute-start
  246.3 18.9 %adam.1 = (f32[3,256,512]{2,1,0:T(8,128)}, f32[1,512,256]{2,1,0:T(8,128)}, f32[4,256,512]{2,1,0:T(8,128)}, f32[4,512,256]{2,1,0:T(8,128)}, f32[4,256]{1,0:T(4,12...) custom-call(f32[3,256,512]{2,1,0:T(8,128)} %get-tuple-element.79.ref, ...), custom_call_target="tpu_custom_call" | custom-call | tf_op jit(solution)/shard_map/adam/pallas_call | solution.py:1637
  265.2 11.3 %norm_totals.1.refs_0_ = f32[16,128]{1,0:T(8,128)} custom-call(f32[16,128]{1,0:T(8,128)} %get-tuple-element.86.tile), custom_call_target="tpu_custom_call" | custom-call | tf_op jit(solution)/shard_map/norm_totals/pallas_call | solution.py:1680
  276.5 0.0 collective-permute-done.2.refs_15_
  276.5 0.0 copy-start
  276.5 0.0 collective-permute-done.1.refs_14_
  276.6 0.0 copy-start.1
  276.6 0.0 collective-permute-done.refs_13_
  276.6 0.0 copy-start.2
  276.6 0.7 copy-done
  277.2 0.1 copy-done.1
  277.3 0.1 copy-done.2
  277.4 10.1 %new_weights.1 = (f32[3,256,512]{2,1,0:T(8,128)}, f32[1,512,256]{2,1,0:T(8,128)}, f32[4,256,512]{2,1,0:T(8,128)}, f32[4,512,256]{2,1,0:T(8,128)}, f32[4,256]{1,0...) custom-call(f32[16,128]{1,0:T(8,128)} %norm_totals.1.refs_0_, ...), custom_call_target="tpu_custom_call" | custom-call | tf_op jit(solution)/shard_map/new_weights/pallas_call | solution.py:1761
Async XLA Ops:
  243.2 33.3 %collective-permute-start.2 = (bf16[64,2048]{1,0:T(8,128)(2,1)}, bf16[64,2048]{1,0:T(8,128)(2,1)S(1)}, u32[]{:S(2)}, u32[]{:S(2)}) collective-permute-start(bf16[64,2048]{1,0:T(8,128)(2,1)} %get-tuple-element.92.refs_12_), channel_id=1, source_target_pairs={{0,3},{1,0},{2,1},{3,2},{4,7},{5,4},{6,5},{7,6},{8,11},{9,8},{10,9... | collective-permute-start | bytes 786440 | tf_op jit(solution)/shard_map/ppermute | solution.py:1866
  245.3 31.3 %collective-permute-start.1 = (bf16[64,2048]{1,0:T(8,128)(2,1)}, bf16[64,2048]{1,0:T(8,128)(2,1)S(1)}, u32[]{:S(2)}, u32[]{:S(2)}) collective-permute-start(bf16[64,2048]{1,0:T(8,128)(2,1)} %get-tuple-element.92.refs_12_), channel_id=1, source_target_pairs={{0,2},{1,3},{2,0},{3,1},{4,6},{5,7},{6,4},{7,5},{8,10},{9,11},{10,... | collective-permute-start | bytes 786440 | tf_op jit(solution)/shard_map/ppermute | solution.py:1866
  245.5 31.1 %collective-permute-start = (bf16[64,2048]{1,0:T(8,128)(2,1)}, bf16[64,2048]{1,0:T(8,128)(2,1)S(1)}, u32[]{:S(2)}, u32[]{:S(2)}) collective-permute-start(bf16[64,2048]{1,0:T(8,128)(2,1)} %get-tuple-element.92.refs_12_), channel_id=1, source_target_pairs={{0,1},{1,2},{2,3},{3,0},{4,5},{5,6},{6,7},{7,4},{8,9},{9,10},{10,1... | collective-permute-start | bytes 786440 | tf_op jit(solution)/shard_map/ppermute | solution.py:1866
  276.5 0.7 copy-start
  276.6 0.8 copy-start.1
  276.6 0.8 copy-start.2
where the time goes:
time: 288 us
  Pallas kernels  282 us (98%)
  starting transfers between devices  3.1 us (1%)
    pallas_call x1, Pallas kernels, front_call(): pl.pallas_call(front_kernel, out_shape=[both, both, jax.ShapeDtypeStruct(...  121 us
    pallas_call x1, Pallas kernels, back_call(): pl.pallas_call(back_kernel, out_shape=[jax.ShapeDtypeStruct((length, widt...  121 us
    pallas_call x1, Pallas kernels, adam_call(): pl.pallas_call(adam_kernel, out_shape=like * 3 + [jax.ShapeDtypeStruct((1...  18.9 us
    pallas_call x1, Pallas kernels, total_call(): pl.pallas_call(total_kernel, out_shape=jax.ShapeDtypeStruct((16, 128), F3...  11.3 us
    pallas_call x1, Pallas kernels, weight_call(): pl.pallas_call(weight_kernel, out_shape=[jax.ShapeDtypeStruct(shape, F32)...  10.1 us
  transfers between devices with their start and end apart: 3, of which 0 were waited for; matrix products, arithmetic and copies ran while one was open for 0% of the time, Pallas kernels for 10%

commit v1 on v0

--- a/solution.py
+++ b/solution.py
@@ -1039,8 +1039,10 @@
 def front_kernel(*refs):
     head_count, position, bucket, tok, cot, norm_master = refs[:6]
     masters = refs[6:10]
-    n1, both_cot, tables, packs, n2, mid, q_out, k_out, v_out, a_out = refs[10:20]
-    wholes = refs[20:24]
+    n1_hbm, both_cot, tables, packs, n2, mid = refs[10:16]
+    homes = [n1_hbm, *refs[16:22]]
+    n1, q_out, k_out, v_out, a_out, wq_all, wo_all, home_sem = refs[58:66]
+    wholes = [wq_all, wo_all, *refs[22:24]]
     raws, shards = refs[24:28], refs[28:32]
     raw_sem, n2_own, part, small, pair, local = refs[32:38]
     sums, tensor_sems, gather_refs = refs[38:43], refs[43:46], refs[46:58]
@@ -1115,6 +1117,14 @@
     total.start()
     attend_out(a_out, wholes[1], part, here.c)
     total.spread()
+    homeward = [
+        pltpu.make_async_copy(src, dst, home_sem.at[i])
+        for i, (src, dst) in enumerate(
+            zip((n1, q_out, k_out, v_out, a_out, wq_all, wo_all), homes)
+        )
+    ]
+    for copy in homeward:
+        copy.start()
     rows = block(here.z, ROWS)
     middle = tok[rows, :].astype(F32) + total.result()
     mid[...] = middle
@@ -1130,6 +1140,8 @@
     gathers[2].finish()
     gathers[3].finish()
     keep.wait()
+    for copy in homeward:
+        copy.wait()
     shared[0].wait_send()
     shared[1].wait()
     shared[2].wait_send()
@@ -1158,7 +1170,7 @@
         ]
         + wholes,
         in_specs=[SM, VM, VM, VM, VM, VM] + [ANY] * 4,
-        out_specs=[VM, ANY, VM, VM, ANY, VM, VM, VM, VM, VM, VM, VM, ANY, ANY],
+        out_specs=[ANY, ANY, VM, VM, ANY, VM] + [ANY] * 8,
         scratch_shapes=[pltpu.VMEM(master.shape, F32) for master in masters]
         + [pltpu.VMEM(master.shape, BF16) for master in masters]
         + [
@@ -1171,7 +1183,11 @@
         ]
         + sum_scratch(length, width)
         + tensor_gather_sems()
-        + gather_sems() * 4,
+        + gather_sems() * 4
+        + [pltpu.VMEM(both.shape, BF16)]
+        + [pltpu.VMEM(thin.shape, BF16)] * 4
+        + [pltpu.VMEM(wholes[0].shape, BF16), pltpu.VMEM(wholes[1].shape, BF16)]
+        + [pltpu.SemaphoreType.DMA((7,))],
         compiler_params=params(1),
         name="front",
     )(head_count, position, bucket, tok, cot, norm_master, *masters)

time: 288 us -> 286 us (level)
  transfers between devices with their start and end apart: 3 -> 3, of which waited for: 0 -> 0; matrix products, arithmetic and copies ran while one was open for 0% -> 0% of each run, Pallas kernels for 10% -> 11%
where the time goes in v1:
time: 286 us; the launch traced here: 285 us
  Pallas kernels  280 us (98%)
  starting transfers between devices  3.36 us (1%)
    pallas_call x1, Pallas kernels, back_call(): pl.pallas_call(back_kernel, out_shape=[jax.ShapeDtypeStruct((length, widt...  121 us
    pallas_call x1, Pallas kernels, front_call(): pl.pallas_call(front_kernel, out_shape=[both, both, jax.ShapeDtypeStruct(...  119 us
    pallas_call x1, Pallas kernels, adam_call(): pl.pallas_call(adam_kernel, out_shape=like * 3 + [jax.ShapeDtypeStruct((1...  18.9 us
    pallas_call x1, Pallas kernels, total_call(): pl.pallas_call(total_kernel, out_shape=jax.ShapeDtypeStruct((16, 128), F3...  11.3 us
    pallas_call x1, Pallas kernels, weight_call(): pl.pallas_call(weight_kernel, out_shape=[jax.ShapeDtypeStruct(shape, F32)...  10.1 us
  transfers between devices with their start and end apart: 3, of which 0 were waited for; matrix products, arithmetic and copies ran while one was open for 0% of the time, Pallas kernels for 11%

profile of v1, /device:TPU:0, one launch (start us, length us, event | category | flops | bytes accessed | tf_op | source)
XLA Modules:
  0.0 285.5 jit_solution(11651454825411775792)
XLA Ops:
  1.3 118.8 %front.1 = (bf16[2,256,2048]{2,1,0:T(8,128)(2,1)}, bf16[2,256,2048]{2,1,0:T(8,128)(2,1)}, f32[2,5,256,128]{3,2,1,0:T(8,128)}, f32[8,8,256]{2,1,0:T(8,128)}, bf16...) custom-call(s32[1]{0:T(128)S(6)} %copy.39.refs_0_, ...), custom_call_target="tpu_custom_call" | custom-call | tf_op jit(solution)/shard_map/front/pallas_call | solution.py:1160
  120.1 120.6 %back.1 = (bf16[256,2048]{1,0:T(8,128)(2,1)}, bf16[64,2048]{1,0:T(8,128)(2,1)}, f32[8,256]{1,0:T(8,128)}, f32[3,256,512]{2,1,0:T(8,128)}, f32[1,512,256]{2,1,0:T...) custom-call(bf16[2,256,2048]{2,1,0:T(8,128)(2,1)} %get-tuple-element.65.refs_0_, ...), custom_call_target="tpu_custom_call" | custom-call | tf_op jit(solution)/shard_map/back/pallas_call | solution.py:1499
  240.7 2.3 collective-permute-start.2
  243.1 0.0 collective-permute-start.1
  243.1 1.0 collective-permute-start
  244.1 18.9 %adam.1 = (f32[3,256,512]{2,1,0:T(8,128)}, f32[1,512,256]{2,1,0:T(8,128)}, f32[4,256,512]{2,1,0:T(8,128)}, f32[4,512,256]{2,1,0:T(8,128)}, f32[4,256]{1,0:T(4,12...) custom-call(f32[3,256,512]{2,1,0:T(8,128)} %get-tuple-element.79.ref, ...), custom_call_target="tpu_custom_call" | custom-call | tf_op jit(solution)/shard_map/adam/pallas_call | solution.py:1653
  263.0 11.3 %norm_totals.1.refs_0_ = f32[16,128]{1,0:T(8,128)} custom-call(f32[16,128]{1,0:T(8,128)} %get-tuple-element.86.tile), custom_call_target="tpu_custom_call" | custom-call | tf_op jit(solution)/shard_map/norm_totals/pallas_call | solution.py:1696
  274.3 0.0 collective-permute-done.2.refs_15_
  274.3 0.0 copy-start
  274.3 0.0 collective-permute-done.1.refs_14_
  274.3 0.0 copy-start.1
  274.3 0.0 collective-permute-done.refs_13_
  274.3 0.0 copy-start.2
  274.3 0.7 copy-done
  275.0 0.1 copy-done.1
  275.1 0.1 copy-done.2
  275.2 10.1 %new_weights.1 = (f32[3,256,512]{2,1,0:T(8,128)}, f32[1,512,256]{2,1,0:T(8,128)}, f32[4,256,512]{2,1,0:T(8,128)}, f32[4,512,256]{2,1,0:T(8,128)}, f32[4,256]{1,0...) custom-call(f32[16,128]{1,0:T(8,128)} %norm_totals.1.refs_0_, ...), custom_call_target="tpu_custom_call" | custom-call | tf_op jit(solution)/shard_map/new_weights/pallas_call | solution.py:1777
Async XLA Ops:
  240.7 33.5 %collective-permute-start.2 = (bf16[64,2048]{1,0:T(8,128)(2,1)}, bf16[64,2048]{1,0:T(8,128)(2,1)S(1)}, u32[]{:S(2)}, u32[]{:S(2)}) collective-permute-start(bf16[64,2048]{1,0:T(8,128)(2,1)} %get-tuple-element.92.refs_12_), channel_id=1, source_target_pairs={{0,3},{1,0},{2,1},{3,2},{4,7},{5,4},{6,5},{7,6},{8,11},{9,8},{10,9... | collective-permute-start | bytes 786440 | tf_op jit(solution)/shard_map/ppermute | solution.py:1882
  243.1 31.2 %collective-permute-start.1 = (bf16[64,2048]{1,0:T(8,128)(2,1)}, bf16[64,2048]{1,0:T(8,128)(2,1)S(1)}, u32[]{:S(2)}, u32[]{:S(2)}) collective-permute-start(bf16[64,2048]{1,0:T(8,128)(2,1)} %get-tuple-element.92.refs_12_), channel_id=1, source_target_pairs={{0,2},{1,3},{2,0},{3,1},{4,6},{5,7},{6,4},{7,5},{8,10},{9,11},{10,... | collective-permute-start | bytes 786440 | tf_op jit(solution)/shard_map/ppermute | solution.py:1882
  243.1 31.3 %collective-permute-start = (bf16[64,2048]{1,0:T(8,128)(2,1)}, bf16[64,2048]{1,0:T(8,128)(2,1)S(1)}, u32[]{:S(2)}, u32[]{:S(2)}) collective-permute-start(bf16[64,2048]{1,0:T(8,128)(2,1)} %get-tuple-element.92.refs_12_), channel_id=1, source_target_pairs={{0,1},{1,2},{2,3},{3,0},{4,5},{5,6},{6,7},{7,4},{8,9},{9,10},{10,1... | collective-permute-start | bytes 786440 | tf_op jit(solution)/shard_map/ppermute | solution.py:1882
  274.3 0.7 copy-start
  274.3 0.8 copy-start.1
  274.3 0.8 copy-start.2
